TPU v7x, 128 devices: a whole 4x4x4 slice. The times are simulated.
128 devices in a mesh: space: 8 (over z, x_hi), ens: 16 (over y, x_lo, core).
Axes of the slice: x: 4 (x_hi: 2, x_lo: 2; x = x_hi * 2 + x_lo), y: 4, z: 4, core: 2. Of those that a mesh axis runs over, the one named last changes fastest.
Arguments:
- log_perm: float32 [128, 16, 64, 512], P('ens', 'space'), may hold values from -4 to 4
- storage: float32 [16, 64, 512], P('space'), may hold values from 0.5 to 2
- head_init: float32 [16, 64, 512], P('space'), may hold values from -6 to 6
- well_cells: int32 [16], replicated, may hold values from 0 to 524287
- well_rates: float32 [16], replicated, may hold values from -12 to 12
- obs_cells: int32 [32], replicated, may hold values from 0 to 524287
- obs_values: float32 [32], replicated, may hold values from -6 to 6
- noise_var: float32 [32], replicated, may hold values from 0.05 to 0.5
- step_size: float32 [1], replicated, may hold values from 0.5 to 2
- perturb: float32 [128, 32], P('ens'), may hold values from -2 to 2
Outputs:
- head_field: float32 [128, 16, 64, 512], P('ens', 'space')
- updated: float32 [128, 16, 64, 512], P('ens', 'space')
All inputs are finite; a program needn't handle non-finite values.
Results may differ from a plain program's by a relative error of at most 0.00025.
Values sent between devices are 32-bit elements; how exact they have to be, the bound alone decides.
A program may use at most 192 MiB of HBM per device.

v0:
```python
import jax
import jax.numpy as jnp
from jax import lax
from jax.sharding import PartitionSpec as P

SWEEPS = 3
OMEGA = 0.8
HIGHEST = lax.Precision.HIGHEST
DIRECTIONS = [
    (a, b, c) for a in (-1, 0, 1) for b in (-1, 0, 1) for c in (-1, 0, 1) if (a, b, c) != (0, 0, 0)
]


def padded_2(block, sides, width):
    for axis, dim in sides:
        count = lax.axis_size(axis)
        forward = [(i, i + 1) for i in range(count - 1)]
        backward = [(target, source) for source, target in forward]
        low = lax.ppermute(
            lax.slice_in_dim(block, block.shape[dim] - width, None, axis=dim), axis, forward
        )
        high = lax.ppermute(lax.slice_in_dim(block, 0, width, axis=dim), axis, backward)
        block = jnp.concatenate([low, block, high], axis=dim)
    return block


def shifted(padded, a, b, c, planes, depth, across):
    return padded[..., 1 + a : 1 + a + planes, 1 + b : 1 + b + depth, 1 + c : 1 + c + across]


def solve_pair(factor, residual):
    first = lax.linalg.triangular_solve(factor, residual.T, left_side=True, lower=True)
    second = lax.linalg.triangular_solve(
        factor, first, left_side=True, lower=True, transpose_a=True
    )
    return second.T


def shards(
    log_perm,
    storage,
    head_init,
    well_cells,
    well_rates,
    obs_cells,
    obs_values,
    noise_var,
    step_size,
    perturb,
):
    members, planes, depth, across = log_perm.shape
    cell_count = planes * depth * across
    total_members = members * lax.axis_size("ens")
    offset = lax.axis_index("space") * cell_count
    cell_ids = lax.broadcasted_iota(jnp.int32, (1, cell_count), 1)
    hits = (cell_ids == (well_cells - offset)[:, None]).astype(jnp.float32)
    source = jnp.dot(well_rates, hits, precision=HIGHEST).reshape(planes, depth, across)
    permeability = jnp.exp(log_perm)
    rimmed = padded_2(permeability, (("space", 1),), 1)
    padded = jnp.pad(rimmed, ((0, 0), (0, 0), (1, 1), (1, 1)))
    transmit = []
    for a, b, c in DIRECTIONS:
        factor = 2.0 ** (1 - abs(a) - abs(b) - abs(c))
        neighbour = shifted(padded, a, b, c, planes, depth, across)
        transmit.append(factor * 2.0 * permeability * neighbour / (permeability + neighbour))
    diagonal = storage + sum(transmit)
    forcing = storage * head_init + source
    head_field = jnp.broadcast_to(head_init, log_perm.shape)
    for sweep_index in range(SWEEPS):
        rimmed_head = padded_2(head_field, (("space", 1),), 1)
        padded_head = jnp.pad(rimmed_head, ((0, 0), (0, 0), (1, 1), (1, 1)))
        gathered = sum(
            (
                transmit[i] * shifted(padded_head, a, b, c, planes, depth, across)
                for i, (a, b, c) in enumerate(DIRECTIONS)
            )
        )
        head_field = (1.0 - OMEGA) * head_field + OMEGA * (forcing + gathered) / diagonal
    local_obs = obs_cells - offset
    inside = ((local_obs >= 0) & (local_obs < cell_count)).astype(jnp.float32)
    picked = (
        jnp.take(
            head_field.reshape(members, cell_count), jnp.clip(local_obs, 0, cell_count - 1), axis=1
        )
        * inside
    )
    observed = lax.psum(picked, "space")
    every_obs = lax.all_gather(observed, "ens", axis=0, tiled=True)
    mean_obs = jnp.mean(every_obs, axis=0)
    spread = every_obs - mean_obs
    covariance = jnp.dot(spread.T, spread, precision=HIGHEST) / (total_members - 1)
    deviation = observed - mean_obs
    system = covariance + jnp.diag(noise_var / step_size[0])
    factor_lower = jnp.linalg.cholesky(system)
    gain_rows = solve_pair(factor_lower, obs_values[None, :] + perturb - observed)
    flat = log_perm.reshape(members, cell_count)
    piece_field = lax.all_gather(flat, "ens", axis=0, tiled=True)
    piece_dev = lax.all_gather(deviation, "ens", axis=0, tiled=True)
    mixing = jnp.dot(piece_dev, gain_rows.T, precision=HIGHEST)
    change = lax.dot_general(mixing, piece_field, (((0,), (0,)), ((), ())), precision=HIGHEST)
    updated = (flat + change / (total_members - 1)).reshape(log_perm.shape)
    return (head_field, updated)


def solution(mesh):
    return jax.shard_map(
        shards,
        mesh=mesh,
        in_specs=(
            P("ens", "space", None, None),
            P("space", None, None),
            P("space", None, None),
            P(),
            P(),
            P(),
            P(),
            P(),
            P(),
            P("ens", None),
        ),
        out_specs=(P("ens", "space", None, None), P("ens", "space", None, None)),
        check_vma=False,
    )
```

profile of v0, /device:TPU:1, one launch (start us, length us, event | category | flops | bytes accessed | tf_op | source)
XLA Modules:
  0.0 545.3 jit_solution(13911891176995488092)
XLA Ops:
  7.2 4.2 copy.30
  14.9 5.7 %collective-permute-start = (f32[8,1,64,512]{3,2,1,0:T(8,128)}, f32[8,1,64,512]{3,2,1,0:T(8,128)S(1)}, u32[]{:S(2)}, u32[]{:S(2)}) collective-permute-start(f32[8,1,64,512]{3,2,1,0:T(8,128)} %get-tuple-element.14), channel_id=1, source_target_pairs={{0,16},{16,32},{32,48},{48,64},{64,80},{80,96},{96,112},{1,17},{17... | collective-permute-start | bytes 3145736 | tf_op jit(solution)/shard_map/ppermute | solution.py:19
  23.1 6.5 %collective-permute-start.2 = (f32[8,1,64,512]{3,2,1,0:T(8,128)}, f32[8,1,64,512]{3,2,1,0:T(8,128)}, u32[]{:S(2)}, u32[]{:S(2)}) collective-permute-start(f32[8,1,64,512]{3,2,1,0:T(8,128)} %broadcast_in_dim.53), channel_id=1, source_target_pairs={{0,16},{16,32},{32,48},{48,64},{64,80},{80,96},{96,112},{1,17},{17... | collective-permute-start | bytes 3145736 | tf_op jit(solution)/shard_map/ppermute | solution.py:19
  37.6 23.5 %collective-permute-done = f32[8,1,64,512]{3,2,1,0:T(8,128)S(1)} collective-permute-done((f32[8,1,64,512]{3,2,1,0:T(8,128)}, f32[8,1,64,512]{3,2,1,0:T(8,128)S(1)}, u32[]{:S(2)}, u32[]{:S(2)}) %collective-permute-start) | collective-permute-done | bytes 1048608 | tf_op jit(solution)/shard_map/ppermute | solution.py:19
  61.1 45.9 %collective-permute-done.1 = f32[8,1,64,512]{3,2,1,0:T(8,128)} collective-permute-done((f32[8,1,64,512]{3,2,1,0:T(8,128)}, f32[8,1,64,512]{3,2,1,0:T(8,128)}, u32[]{:S(2)}, u32[]{:S(2)}) %collective-permute-start.1) | collective-permute-done | bytes 1048608 | tf_op jit(solution)/shard_map/ppermute | solution.py:22
  107.0 3.7 select_maximum_fusion.6
  110.7 86.2 %collective-permute-done.3 = f32[8,1,64,512]{3,2,1,0:T(8,128)} collective-permute-done((f32[8,1,64,512]{3,2,1,0:T(8,128)}, f32[8,1,64,512]{3,2,1,0:T(8,128)}, u32[]{:S(2)}, u32[]{:S(2)}) %collective-permute-start.3) | collective-permute-done | bytes 1048608 | tf_op jit(solution)/shard_map/ppermute | solution.py:22
  197.2 4.7 select_maximum_fusion.4
  201.9 23.9 %fusion.71 = f32[8,2,64,512]{3,2,1,0:T(8,128)} fusion(f32[8,4,66,514]{3,2,1,0:T(8,128)S(1)} %select_maximum_fusion.4, f32[8,1,64,512]{3,2,1,0:T(8,128)} %collective-permute-done.3, f32[8,2,64,512]{3,2,1,0:T(8,128)} %copy-done.5, f32[8,1,64,512]{3,2,1,0:T(8,128)} %collective-permute-done.2, f32[2,64,512]{2,1,0:T(8,128)S(1)} %copy-done.7, ...), kind=kLoop, calls=%fused_computation.139 | loop fusion | flops 87031808 | bytes 114032640 | tf_op jit(solution)/shard_map/add | solution.py:78
  227.7 6.2 %collective-permute-start.4 = (f32[8,1,64,512]{3,2,1,0:T(8,128)S(1)}, f32[8,1,64,512]{3,2,1,0:T(8,128)S(1)}, u32[]{:S(2)}, u32[]{:S(2)}) collective-permute-start(f32[8,1,64,512]{3,2,1,0:T(8,128)S(1)} %get-tuple-element.12), channel_id=1, source_target_pairs={{0,16},{16,32},{32,48},{48,64},{64,80},{80,96},{96,112},{1,17},{17... | collective-permute-start | bytes 3145736 | tf_op jit(solution)/shard_map/ppermute | solution.py:19
  235.5 16.8 %collective-permute-done.4 = f32[8,1,64,512]{3,2,1,0:T(8,128)S(1)} collective-permute-done((f32[8,1,64,512]{3,2,1,0:T(8,128)S(1)}, f32[8,1,64,512]{3,2,1,0:T(8,128)S(1)}, u32[]{:S(2)}, u32[]{:S(2)}) %collective-permute-start.4) | collective-permute-done | bytes 1048608 | tf_op jit(solution)/shard_map/ppermute | solution.py:19
  252.3 62.0 %collective-permute-done.5 = f32[8,1,64,512]{3,2,1,0:T(8,128)S(1)} collective-permute-done((f32[8,1,64,512]{3,2,1,0:T(8,128)S(1)}, f32[8,1,64,512]{3,2,1,0:T(8,128)S(1)}, u32[]{:S(2)}, u32[]{:S(2)}) %collective-permute-start.5) | collective-permute-done | bytes 1048608 | tf_op jit(solution)/shard_map/ppermute | solution.py:22
  317.9 22.7 %fusion.40 = f32[8,2,64,512]{3,2,1,0:T(8,128)} fusion(f32[8,4,66,514]{3,2,1,0:T(8,128)S(1)} %select_maximum_fusion.2, f32[8,1,64,512]{3,2,1,0:T(8,128)} %copy-done.9, f32[8,2,64,512]{3,2,1,0:T(8,128)} %fusion.71, f32[8,1,64,512]{3,2,1,0:T(8,128)S(1)} %collective-permute-done.4, f32[2,64,512]{2,1,0:T(8,128)S(1)} %copy-done.7, ...), kind=kLoop, calls=%fused_computation.82 | loop fusion | flops 87556096 | bytes 113770496 | tf_op jit(solution)/shard_map/add | solution.py:78
  342.5 4.7 collective-permute-start.6
  349.2 18.5 %collective-permute-done.6 = f32[8,1,64,512]{3,2,1,0:T(8,128)S(1)} collective-permute-done((f32[8,1,64,512]{3,2,1,0:T(8,128)S(1)}, f32[8,1,64,512]{3,2,1,0:T(8,128)S(1)}, u32[]{:S(2)}, u32[]{:S(2)}) %collective-permute-start.6) | collective-permute-done | bytes 1048608 | tf_op jit(solution)/shard_map/ppermute | solution.py:19
  367.7 25.0 %collective-permute-done.7 = f32[8,1,64,512]{3,2,1,0:T(8,128)S(1)} collective-permute-done((f32[8,1,64,512]{3,2,1,0:T(8,128)S(1)}, f32[8,1,64,512]{3,2,1,0:T(8,128)S(1)}, u32[]{:S(2)}, u32[]{:S(2)}) %collective-permute-start.7) | collective-permute-done | bytes 1048608 | tf_op jit(solution)/shard_map/ppermute | solution.py:22
  396.3 22.7 %fusion.9 = f32[8,2,64,512]{3,2,1,0:T(8,128)} fusion(f32[8,4,66,514]{3,2,1,0:T(8,128)S(1)} %select_maximum_fusion, f32[8,1,64,512]{3,2,1,0:T(8,128)} %copy-done.8, f32[8,2,64,512]{3,2,1,0:T(8,128)} %fusion.40, f32[8,1,64,512]{3,2,1,0:T(8,128)S(1)} %collective-permute-done.6, f32[2,64,512]{2,1,0:T(8,128)S(1)} %copy-done.7, ...), kind=kLoop, calls=%fused_computation.25 | loop fusion | flops 87556096 | bytes 113770496 | tf_op jit(solution)/shard_map/add | solution.py:78
  419.0 18.0 %copy.24 = f32[8,2,64,512]{0,3,2,1:T(8,128)} copy(f32[8,2,64,512]{3,2,1,0:T(8,128)} %fusion.9) | data formatting | bytes 4194304 | tf_op jit(solution)/shard_map/add | solution.py:78
  437.0 11.1 %gather_fusion = f32[32,8]{1,0:T(8,128)S(1)} fusion(f32[8,65536]{0,1:T(8,128)} %bitcast.36, s32[1024]{0:T(1024)S(1)} %pad_clamp_fusion), kind=kCustom, calls=%fused_computation | custom fusion | bytes 2176 | tf_op jit(solution)/shard_map/jit(_take)/gather | solution.py:82
  448.2 18.1 %psum.7 = f32[8,32]{1,0:T(8,128)S(1)} all-reduce(f32[8,32]{1,0:T(8,128)S(1)} %multiply_bitcast_fusion), channel_id=1, replica_groups=mesh['space'=8,'ens'=16] {'space'}, use_global_device_ids=true, to_apply=%region_0.1 | all-reduce | flops 256 | bytes 2048 | tf_op jit(solution)/shard_map/psum | solution.py:87
  466.3 25.5 %all_gather.9 = f32[128,32]{1,0:T(8,128)S(1)} all-gather(f32[8,32]{1,0:T(8,128)S(1)} %psum.7), channel_id=1, replica_groups=mesh['space'=8,'ens'=16] {'ens'}, dimensions={0}, use_global_device_ids=true | all-gather | bytes 17408 | tf_op jit(solution)/shard_map/all_gather | solution.py:88
  492.3 2.9 cholesky.16
  499.0 16.7 %all_gather.10 = f32[128,32]{1,0:T(8,128)S(1)} all-gather(f32[8,32]{1,0:T(8,128)S(1)} %broadcast_subtract_fusion), channel_id=1, replica_groups=mesh['space'=8,'ens'=16] {'ens'}, dimensions={0}, use_global_device_ids=true | all-gather | bytes 17408 | tf_op jit(solution)/shard_map/all_gather | solution.py:98
  516.3 19.6 %fusion = f32[8,65536]{1,0:T(8,128)S(1)} fusion(f32[8,65536]{1,0:T(8,128)S(1)} %bitcast.38, f32[128,8]{0,1:T(8,128)S(1)} %fusion.121, f32[128,65536]{1,0:T(8,128)} %all-gather.2.cloned.1.call-done), kind=kOutput, calls=%fused_computation.2 | convolution fusion | flops 806354944 | bytes 37752832 | tf_op jit(solution)/shard_map/dot_general | solution.py:100
  (75 shorter events, 35.5 us)
Async XLA Ops:
  7.2 24.9 %copy-start = (f32[16]{0:T(128)S(1)}, f32[16]{0:T(128)}, u32[]{:S(2)}) copy-start(f32[16]{0:T(128)} %param.14) | copy-start | bytes 196
  7.2 509.1 %all-gather.2.cloned.1.call-start = ((), (), s32[]{:S(2)}) async-start(), calls=%async_computation | async-start | bytes 35651584 | tf_op jit(solution)/shard_map/all_gather | solution.py:97
  13.4 8.7 %copy-start.10 = (f32[2,64,512]{2,1,0:T(8,128)S(1)}, f32[2,64,512]{2,1,0:T(8,128)}, u32[]{:S(2)}) copy-start(f32[2,64,512]{2,1,0:T(8,128)} %param.12) | copy-start | bytes 786436
  14.9 17.1 %copy-start.15 = (s32[16]{0:T(128)S(1)}, s32[16]{0:T(128)}, u32[]{:S(2)}) copy-start(s32[16]{0:T(128)} %param.13) | copy-start | bytes 196
  14.9 46.2 %collective-permute-start = (f32[8,1,64,512]{3,2,1,0:T(8,128)}, f32[8,1,64,512]{3,2,1,0:T(8,128)S(1)}, u32[]{:S(2)}, u32[]{:S(2)}) collective-permute-start(f32[8,1,64,512]{3,2,1,0:T(8,128)} %get-tuple-element.14), channel_id=1, source_target_pairs={{0,16},{16,32},{32,48},{48,64},{64,80},{80,96},{96,112},{1,17},{17... | collective-permute-start | bytes 3145736 | tf_op jit(solution)/shard_map/ppermute | solution.py:19
  20.6 15.3 %copy-start.7 = (f32[2,64,512]{2,1,0:T(8,128)S(1)}, f32[2,64,512]{2,1,0:T(8,128)}, u32[]{:S(2)}) copy-start(f32[2,64,512]{2,1,0:T(8,128)} %param.11) | copy-start | bytes 786436
  20.6 86.4 %collective-permute-start.1 = (f32[8,1,64,512]{3,2,1,0:T(8,128)}, f32[8,1,64,512]{3,2,1,0:T(8,128)}, u32[]{:S(2)}, u32[]{:S(2)}) collective-permute-start(f32[8,1,64,512]{3,2,1,0:T(8,128)} %get-tuple-element.15), channel_id=1, source_target_pairs={{16,0},{32,16},{48,32},{64,48},{80,64},{96,80},{112,96},{17,1},{33... | collective-permute-start | bytes 3145736 | tf_op jit(solution)/shard_map/ppermute | solution.py:22
  23.1 87.6 %collective-permute-start.2 = (f32[8,1,64,512]{3,2,1,0:T(8,128)}, f32[8,1,64,512]{3,2,1,0:T(8,128)}, u32[]{:S(2)}, u32[]{:S(2)}) collective-permute-start(f32[8,1,64,512]{3,2,1,0:T(8,128)} %broadcast_in_dim.53), channel_id=1, source_target_pairs={{0,16},{16,32},{32,48},{48,64},{64,80},{80,96},{96,112},{1,17},{17... | collective-permute-start | bytes 3145736 | tf_op jit(solution)/shard_map/ppermute | solution.py:19
  30.7 166.1 %collective-permute-start.3 = (f32[8,1,64,512]{3,2,1,0:T(8,128)}, f32[8,1,64,512]{3,2,1,0:T(8,128)}, u32[]{:S(2)}, u32[]{:S(2)}) collective-permute-start(f32[8,1,64,512]{3,2,1,0:T(8,128)} %broadcast_in_dim.55), channel_id=1, source_target_pairs={{16,0},{32,16},{48,32},{64,48},{80,64},{96,80},{112,96},{17,1},{33... | collective-permute-start | bytes 3145736 | tf_op jit(solution)/shard_map/ppermute | solution.py:22
  37.6 159.3 %copy-start.11 = (f32[2,64,512]{2,1,0:T(8,128)S(1)}, f32[2,64,512]{2,1,0:T(8,128)}, u32[]{:S(2)}) copy-start(f32[2,64,512]{2,1,0:T(8,128)} %param.12) | copy-start | bytes 786436
  197.1 4.7 copy-start.5
  197.2 4.7 copy-start.2
  225.8 89.4 %copy-start.4 = (f32[8,2,64,512]{3,2,1,0:T(8,128)S(1)}, f32[8,2,64,512]{3,2,1,0:T(8,128)}, u32[]{:S(2)}) copy-start(f32[8,2,64,512]{3,2,1,0:T(8,128)} %fusion.71) | copy-start | bytes 6291460
  227.7 24.5 %collective-permute-start.4 = (f32[8,1,64,512]{3,2,1,0:T(8,128)S(1)}, f32[8,1,64,512]{3,2,1,0:T(8,128)S(1)}, u32[]{:S(2)}, u32[]{:S(2)}) collective-permute-start(f32[8,1,64,512]{3,2,1,0:T(8,128)S(1)} %get-tuple-element.12), channel_id=1, source_target_pairs={{0,16},{16,32},{32,48},{48,64},{64,80},{80,96},{96,112},{1,17},{17... | collective-permute-start | bytes 3145736 | tf_op jit(solution)/shard_map/ppermute | solution.py:19
  234.0 80.3 %collective-permute-start.5 = (f32[8,1,64,512]{3,2,1,0:T(8,128)S(1)}, f32[8,1,64,512]{3,2,1,0:T(8,128)S(1)}, u32[]{:S(2)}, u32[]{:S(2)}) collective-permute-start(f32[8,1,64,512]{3,2,1,0:T(8,128)S(1)} %get-tuple-element.13), channel_id=1, source_target_pairs={{16,0},{32,16},{48,32},{64,48},{80,64},{96,80},{112,96},{17,1},{33... | collective-permute-start | bytes 3145736 | tf_op jit(solution)/shard_map/ppermute | solution.py:22
  340.6 8.5 %copy-start.14 = (s32[32]{0:T(128)S(1)}, s32[32]{0:T(128)}, u32[]{:S(2)}) copy-start(s32[32]{0:T(128)} %param.15) | copy-start | bytes 388
  340.6 8.6 %copy-start.16 = (f32[32]{0:T(128)S(1)}, f32[32]{0:T(128)}, u32[]{:S(2)}) copy-start(f32[32]{0:T(128)} %param.17) | copy-start | bytes 388
  340.6 53.0 %copy-start.3 = (f32[8,2,64,512]{3,2,1,0:T(8,128)S(1)}, f32[8,2,64,512]{3,2,1,0:T(8,128)}, u32[]{:S(2)}) copy-start(f32[8,2,64,512]{3,2,1,0:T(8,128)} %fusion.40) | copy-start | bytes 6291460
  342.5 25.2 %collective-permute-start.6 = (f32[8,1,64,512]{3,2,1,0:T(8,128)S(1)}, f32[8,1,64,512]{3,2,1,0:T(8,128)S(1)}, u32[]{:S(2)}, u32[]{:S(2)}) collective-permute-start(f32[8,1,64,512]{3,2,1,0:T(8,128)S(1)} %get-tuple-element.10), channel_id=1, source_target_pairs={{0,16},{16,32},{32,48},{48,64},{64,80},{80,96},{96,112},{1,17},{17... | collective-permute-start | bytes 3145736 | tf_op jit(solution)/shard_map/ppermute | solution.py:19
  347.2 45.5 %collective-permute-start.7 = (f32[8,1,64,512]{3,2,1,0:T(8,128)S(1)}, f32[8,1,64,512]{3,2,1,0:T(8,128)S(1)}, u32[]{:S(2)}, u32[]{:S(2)}) collective-permute-start(f32[8,1,64,512]{3,2,1,0:T(8,128)S(1)} %get-tuple-element.11), channel_id=1, source_target_pairs={{16,0},{32,16},{48,32},{64,48},{80,64},{96,80},{112,96},{17,1},{33... | collective-permute-start | bytes 3145736 | tf_op jit(solution)/shard_map/ppermute | solution.py:22
  419.0 96.8 %copy-start.12 = (f32[8,32]{1,0:T(8,128)S(1)}, f32[8,32]{1,0:T(8,128)}, u32[]{:S(2)}) copy-start(f32[8,32]{1,0:T(8,128)} %param.19) | copy-start | bytes 3076
  419.0 96.8 %copy-start.13 = (f32[32]{0:T(128)S(1)}, f32[32]{0:T(128)}, u32[]{:S(2)}) copy-start(f32[32]{0:T(128)} %param.16) | copy-start | bytes 388
  419.0 97.3 %copy-start.6 = (f32[1,8,128,512]{3,1,2,0:T(8,128)S(1)}, f32[1,8,128,512]{3,1,2,0:T(8,128)}, u32[]{:S(2)}) copy-start(f32[1,8,128,512]{3,1,2,0:T(8,128)} %copy.30) | copy-start | bytes 6291460
  535.9 2.6 copy-start.1
  (2 other events, 1.9 us)
Sparse Core Ops, SparseCore 0:
  11.5 214.9 all-gather.1
where the time goes:
time: 546 us; the launch traced here: 545 us
  waiting for transfers between devices  278 us (51%)
  other arithmetic  91.6 us (17%)
  blocking collectives  60.4 us (11%)
  local copies, waits for them, and re-layouts  49.4 us (9%)
  starting transfers between devices  28.5 us (5%)
  matrix products  22.4 us (4%)
  between operations  15 us (3%)
    ppermute x4, waiting for transfers between devices, padded_2(): lax.ppermute(lax.slice_in_dim(block, 0, width, axis=dim), axis, backward)  219 us
    add x3, other arithmetic, shards(): (1.0 - OMEGA) * head_field + OMEGA * (forcing + gathered) / diagonal  69.3 us
    ppermute x4, waiting for transfers between devices, padded_2(): lax.ppermute(lax.slice_in_dim(block, block.shape[dim] - width, None, axis...  58.8 us
    all_gather x1, blocking collectives, shards(): every_obs = lax.all_gather(observed, 'ens', axis=0, tiled=True)  25.5 us
    ppermute x4, starting transfers between devices, padded_2(): lax.ppermute(lax.slice_in_dim(block, block.shape[dim] - width, None, axis...  23 us
    dot_general x1, matrix products, shards(): lax.dot_general(mixing, piece_field, (((0,), (0,)), ((), ())), precision=...  19.6 us
    psum x1, blocking collectives, shards(): observed = lax.psum(picked, 'space')  18.1 us
    add x1, local copies, waits for them, and re-layouts, shards(): (1.0 - OMEGA) * head_field + OMEGA * (forcing + gathered) / diagonal  18 us
  transfers between devices with their start and end apart: 9, of which 7 were waited for; matrix products, arithmetic and copies ran while one was open for 25% of the time, Pallas kernels for 0%

commit v1 on v0

--- a/solution.py
+++ b/solution.py
@@ -9,6 +9,12 @@
 DIRECTIONS = [
     (a, b, c) for a in (-1, 0, 1) for b in (-1, 0, 1) for c in (-1, 0, 1) if (a, b, c) != (0, 0, 0)
 ]
+
+
+def members_all_bring(shard_in, z):
+    after = jnp.concatenate([shard_in, z], axis=1)
+    left_arr = jax.lax.all_gather(after, axis_name="ens", axis=0, tiled=True)
+    return jnp.split(left_arr, [shard_in.shape[1]], axis=1)
 
 
 def padded_2(block, sides, width):
@@ -94,8 +100,7 @@
     factor_lower = jnp.linalg.cholesky(system)
     gain_rows = solve_pair(factor_lower, obs_values[None, :] + perturb - observed)
     flat = log_perm.reshape(members, cell_count)
-    piece_field = lax.all_gather(flat, "ens", axis=0, tiled=True)
-    piece_dev = lax.all_gather(deviation, "ens", axis=0, tiled=True)
+    piece_field, piece_dev = members_all_bring(flat, deviation)
     mixing = jnp.dot(piece_dev, gain_rows.T, precision=HIGHEST)
     change = lax.dot_general(mixing, piece_field, (((0,), (0,)), ((), ())), precision=HIGHEST)
     updated = (flat + change / (total_members - 1)).reshape(log_perm.shape)

time: 546 us -> 566 us (1.037)
  waiting for transfers between devices: 278 us -> 296 us
  starting transfers between devices: 28.5 us -> 45.8 us
  blocking collectives: 60.4 us -> 43.8 us
    all_gather x1, waiting for transfers between devices: 0.01 us -> 159 us  [members_all_bring(): left_arr = jax.lax.all_gather(after, axis_name='ens', axis=0, tiled=True)]
    ppermute x4, waiting for transfers between devices: 219 us -> 97 us  [padded_2(): lax.ppermute(lax.slice_in_dim(block, 0, width, axis=dim), axis, backward)]
    ppermute x4, waiting for transfers between devices: 58.8 us -> 39.7 us  [padded_2(): lax.ppermute(lax.slice_in_dim(block, block.shape[dim] - width, None, axis...]
    ppermute x4, starting transfers between devices: 23 us -> 40.3 us  [padded_2(): lax.ppermute(lax.slice_in_dim(block, block.shape[dim] - width, None, axis...]
    all_gather x1 -> x0, blocking collectives: 16.7 us -> none  [shards(): piece_dev = lax.all_gather(deviation, 'ens', axis=0, tiled=True)]
  transfers between devices with their start and end apart: 9 -> 9, of which waited for: 7 -> 8; matrix products, arithmetic and copies ran while one was open for 25% -> 4% of each run, Pallas kernels for 0% -> 0%
where the time goes in v1:
time: 566 us; the launch traced here: 565 us
  waiting for transfers between devices  296 us (52%)
  other arithmetic  93.2 us (16%)
  local copies, waits for them, and re-layouts  47.7 us (8%)
  starting transfers between devices  45.8 us (8%)
  blocking collectives  43.8 us (8%)
  matrix products  23.4 us (4%)
  between operations  15 us (3%)
    all_gather x1, waiting for transfers between devices, members_all_bring(): left_arr = jax.lax.all_gather(after, axis_name='ens', axis=0, tiled=True)  159 us
    ppermute x4, waiting for transfers between devices, padded_2(): lax.ppermute(lax.slice_in_dim(block, 0, width, axis=dim), axis, backward)  97 us
    add x3, other arithmetic, shards(): (1.0 - OMEGA) * head_field + OMEGA * (forcing + gathered) / diagonal  69.4 us
    ppermute x4, starting transfers between devices, padded_2(): lax.ppermute(lax.slice_in_dim(block, block.shape[dim] - width, None, axis...  40.3 us
    ppermute x4, waiting for transfers between devices, padded_2(): lax.ppermute(lax.slice_in_dim(block, block.shape[dim] - width, None, axis...  39.7 us
    all_gather x1, blocking collectives, shards(): every_obs = lax.all_gather(observed, 'ens', axis=0, tiled=True)  26.4 us
    dot_general x1, matrix products, shards(): lax.dot_general(mixing, piece_field, (((0,), (0,)), ((), ())), precision=...  19.6 us
    add x1, local copies, waits for them, and re-layouts, shards(): (1.0 - OMEGA) * head_field + OMEGA * (forcing + gathered) / diagonal  18 us
  transfers between devices with their start and end apart: 9, of which 8 were waited for; matrix products, arithmetic and copies ran while one was open for 4% of the time, Pallas kernels for 0%

profile of v1, /device:TPU:1, one launch (start us, length us, event | category | flops | bytes accessed | tf_op | source)
XLA Modules:
  0.0 564.7 jit_solution(7277823546648534783)
XLA Ops:
  10.8 5.7 %collective-permute-start = (f32[8,1,64,512]{3,2,1,0:T(8,128)}, f32[8,1,64,512]{3,2,1,0:T(8,128)S(1)}, u32[]{:S(2)}, u32[]{:S(2)}) collective-permute-start(f32[8,1,64,512]{3,2,1,0:T(8,128)} %get-tuple-element.10), channel_id=1, source_target_pairs={{0,16},{16,32},{32,48},{48,64},{64,80},{80,96},{96,112},{1,17},{17... | collective-permute-start | bytes 3145736 | tf_op jit(solution)/shard_map/ppermute | solution.py:25
  21.4 7.1 %collective-permute-start.2 = (f32[8,1,64,512]{3,2,1,0:T(8,128)}, f32[8,1,64,512]{3,2,1,0:T(8,128)}, u32[]{:S(2)}, u32[]{:S(2)}) collective-permute-start(f32[8,1,64,512]{3,2,1,0:T(8,128)} %broadcast_in_dim.53), channel_id=1, source_target_pairs={{0,16},{16,32},{32,48},{48,64},{64,80},{80,96},{96,112},{1,17},{17... | collective-permute-start | bytes 3145736 | tf_op jit(solution)/shard_map/ppermute | solution.py:25
  34.2 4.3 collective-permute-done
  38.5 24.8 %collective-permute-done.1 = f32[8,1,64,512]{3,2,1,0:T(8,128)} collective-permute-done((f32[8,1,64,512]{3,2,1,0:T(8,128)}, f32[8,1,64,512]{3,2,1,0:T(8,128)}, u32[]{:S(2)}, u32[]{:S(2)}) %collective-permute-start.1) | collective-permute-done | bytes 1048608 | tf_op jit(solution)/shard_map/ppermute | solution.py:28
  63.3 3.7 select_maximum_fusion.6
  67.0 18.8 %collective-permute-done.3 = f32[8,1,64,512]{3,2,1,0:T(8,128)} collective-permute-done((f32[8,1,64,512]{3,2,1,0:T(8,128)}, f32[8,1,64,512]{3,2,1,0:T(8,128)}, u32[]{:S(2)}, u32[]{:S(2)}) %collective-permute-start.3) | collective-permute-done | bytes 1048608 | tf_op jit(solution)/shard_map/ppermute | solution.py:28
  86.1 4.7 select_maximum_fusion.4
  90.8 23.9 %fusion.72 = f32[8,2,64,512]{3,2,1,0:T(8,128)} fusion(f32[8,4,66,514]{3,2,1,0:T(8,128)S(1)} %select_maximum_fusion.4, f32[8,1,64,512]{3,2,1,0:T(8,128)} %collective-permute-done.3, f32[8,2,64,512]{3,2,1,0:T(8,128)} %copy-done.5, f32[8,1,64,512]{3,2,1,0:T(8,128)} %collective-permute-done.2, f32[2,64,512]{2,1,0:T(8,128)S(1)} %copy-done.7, ...), kind=kLoop, calls=%fused_computation.141 | loop fusion | flops 87031808 | bytes 114032640 | tf_op jit(solution)/shard_map/add | solution.py:84
  116.6 23.7 %collective-permute-start.4 = (f32[8,1,64,512]{3,2,1,0:T(8,128)S(1)}, f32[8,1,64,512]{3,2,1,0:T(8,128)S(1)}, u32[]{:S(2)}, u32[]{:S(2)}) collective-permute-start(f32[8,1,64,512]{3,2,1,0:T(8,128)S(1)} %get-tuple-element.8), channel_id=1, source_target_pairs={{0,16},{16,32},{32,48},{48,64},{64,80},{80,96},{96,112},{1,17},{17... | collective-permute-start | bytes 3145736 | tf_op jit(solution)/shard_map/ppermute | solution.py:25
  141.8 19.3 %collective-permute-done.4 = f32[8,1,64,512]{3,2,1,0:T(8,128)S(1)} collective-permute-done((f32[8,1,64,512]{3,2,1,0:T(8,128)S(1)}, f32[8,1,64,512]{3,2,1,0:T(8,128)S(1)}, u32[]{:S(2)}, u32[]{:S(2)}) %collective-permute-start.4) | collective-permute-done | bytes 1048608 | tf_op jit(solution)/shard_map/ppermute | solution.py:25
  161.1 27.8 %collective-permute-done.5 = f32[8,1,64,512]{3,2,1,0:T(8,128)S(1)} collective-permute-done((f32[8,1,64,512]{3,2,1,0:T(8,128)S(1)}, f32[8,1,64,512]{3,2,1,0:T(8,128)S(1)}, u32[]{:S(2)}, u32[]{:S(2)}) %collective-permute-start.5) | collective-permute-done | bytes 1048608 | tf_op jit(solution)/shard_map/ppermute | solution.py:28
  189.9 2.7 select_maximum_fusion.2
  192.6 22.7 %fusion.41 = f32[8,2,64,512]{3,2,1,0:T(8,128)} fusion(f32[8,4,66,514]{3,2,1,0:T(8,128)S(1)} %select_maximum_fusion.2, f32[8,1,64,512]{3,2,1,0:T(8,128)} %copy-done.9, f32[8,2,64,512]{3,2,1,0:T(8,128)} %fusion.72, f32[8,1,64,512]{3,2,1,0:T(8,128)S(1)} %collective-permute-done.4, f32[2,64,512]{2,1,0:T(8,128)S(1)} %copy-done.7, ...), kind=kLoop, calls=%fused_computation.84 | loop fusion | flops 87556096 | bytes 113770496 | tf_op jit(solution)/shard_map/add | solution.py:84
  217.1 3.8 collective-permute-start.6
  224.7 16.0 %collective-permute-done.6 = f32[8,1,64,512]{3,2,1,0:T(8,128)S(1)} collective-permute-done((f32[8,1,64,512]{3,2,1,0:T(8,128)S(1)}, f32[8,1,64,512]{3,2,1,0:T(8,128)S(1)}, u32[]{:S(2)}, u32[]{:S(2)}) %collective-permute-start.6) | collective-permute-done | bytes 1048608 | tf_op jit(solution)/shard_map/ppermute | solution.py:25
  240.8 25.7 %collective-permute-done.7 = f32[8,1,64,512]{3,2,1,0:T(8,128)S(1)} collective-permute-done((f32[8,1,64,512]{3,2,1,0:T(8,128)S(1)}, f32[8,1,64,512]{3,2,1,0:T(8,128)S(1)}, u32[]{:S(2)}, u32[]{:S(2)}) %collective-permute-start.7) | collective-permute-done | bytes 1048608 | tf_op jit(solution)/shard_map/ppermute | solution.py:28
  270.1 22.8 %fusion.10 = f32[8,2,64,512]{3,2,1,0:T(8,128)} fusion(f32[8,4,66,514]{3,2,1,0:T(8,128)S(1)} %select_maximum_fusion, f32[8,1,64,512]{3,2,1,0:T(8,128)} %copy-done.8, f32[8,2,64,512]{3,2,1,0:T(8,128)} %fusion.41, f32[8,1,64,512]{3,2,1,0:T(8,128)S(1)} %collective-permute-done.6, f32[2,64,512]{2,1,0:T(8,128)S(1)} %copy-done.7, ...), kind=kLoop, calls=%fused_computation.27 | loop fusion | flops 87556096 | bytes 113770496 | tf_op jit(solution)/shard_map/add | solution.py:84
  292.9 18.0 %copy.12 = f32[8,2,64,512]{0,3,2,1:T(8,128)} copy(f32[8,2,64,512]{3,2,1,0:T(8,128)} %fusion.10) | data formatting | bytes 4194304 | tf_op jit(solution)/shard_map/add | solution.py:84
  310.9 11.1 %gather_fusion = f32[32,8]{1,0:T(8,128)S(1)} fusion(f32[8,65536]{0,1:T(8,128)} %bitcast.34, s32[1024]{0:T(1024)S(1)} %pad_clamp_fusion), kind=kCustom, calls=%fused_computation | custom fusion | bytes 2176 | tf_op jit(solution)/shard_map/jit(_take)/gather | solution.py:88
  322.1 17.4 %psum.7 = f32[8,32]{1,0:T(8,128)S(1)} all-reduce(f32[8,32]{1,0:T(8,128)S(1)} %multiply_bitcast_fusion), channel_id=1, replica_groups=mesh['space'=8,'ens'=16] {'space'}, use_global_device_ids=true, to_apply=%region_0.1 | all-reduce | flops 256 | bytes 2048 | tf_op jit(solution)/shard_map/psum | solution.py:93
  339.5 26.4 %all_gather.6 = f32[128,32]{1,0:T(8,128)S(1)} all-gather(f32[8,32]{1,0:T(8,128)S(1)} %psum.7), channel_id=1, replica_groups=mesh['space'=8,'ens'=16] {'ens'}, dimensions={0}, use_global_device_ids=true | all-gather | bytes 17408 | tf_op jit(solution)/shard_map/all_gather | solution.py:94
  368.5 2.9 cholesky.16
  375.6 159.0 %all-gather.2.cloned.1.call-done = f32[128,65568]{1,0:T(8,128)} async-done(((f32[8,65568]{1,0:T(8,128)}), f32[128,65568]{1,0:T(8,128)}) %all-gather.2.cloned.1.call-update) | async-done | bytes 33570832 | tf_op jit(solution)/shard_map/all_gather | solution.py:16
  535.7 19.6 %fusion = f32[8,65536]{1,0:T(8,128)S(1)} fusion(f32[8,65536]{1,0:T(8,128)S(1)} %bitcast.36, f32[128,8]{1,0:T(8,128)S(1)} %fusion.106, f32[128,65568]{1,0:T(8,128)} %all-gather.2.cloned.1.call-done), kind=kOutput, calls=%fused_computation.2 | convolution fusion | flops 806354944 | bytes 37752832 | tf_op jit(solution)/shard_map/dot_general | solution.py:105
  (75 shorter events, 37.7 us)
Async XLA Ops:
  7.2 21.4 %copy-start = (f32[16]{0:T(128)S(1)}, f32[16]{0:T(128)}, u32[]{:S(2)}) copy-start(f32[16]{0:T(128)} %param.14) | copy-start | bytes 196
  7.2 527.5 %all-gather.2.cloned.1.call-start = ((), (), s32[]{:S(2)}) async-start(), calls=%async_computation | async-start | bytes 35721216 | tf_op jit(solution)/shard_map/all_gather | solution.py:16
  9.2 8.7 %copy-start.10 = (f32[2,64,512]{2,1,0:T(8,128)S(1)}, f32[2,64,512]{2,1,0:T(8,128)}, u32[]{:S(2)}) copy-start(f32[2,64,512]{2,1,0:T(8,128)} %param.12) | copy-start | bytes 786436
  10.8 17.8 %copy-start.15 = (s32[16]{0:T(128)S(1)}, s32[16]{0:T(128)}, u32[]{:S(2)}) copy-start(s32[16]{0:T(128)} %param.13) | copy-start | bytes 196
  10.8 27.7 %collective-permute-start = (f32[8,1,64,512]{3,2,1,0:T(8,128)}, f32[8,1,64,512]{3,2,1,0:T(8,128)S(1)}, u32[]{:S(2)}, u32[]{:S(2)}) collective-permute-start(f32[8,1,64,512]{3,2,1,0:T(8,128)} %get-tuple-element.10), channel_id=1, source_target_pairs={{0,16},{16,32},{32,48},{48,64},{64,80},{80,96},{96,112},{1,17},{17... | collective-permute-start | bytes 3145736 | tf_op jit(solution)/shard_map/ppermute | solution.py:25
  16.4 15.9 %copy-start.7 = (f32[2,64,512]{2,1,0:T(8,128)S(1)}, f32[2,64,512]{2,1,0:T(8,128)}, u32[]{:S(2)}) copy-start(f32[2,64,512]{2,1,0:T(8,128)} %param.11) | copy-start | bytes 786436
  16.5 46.8 %collective-permute-start.1 = (f32[8,1,64,512]{3,2,1,0:T(8,128)}, f32[8,1,64,512]{3,2,1,0:T(8,128)}, u32[]{:S(2)}, u32[]{:S(2)}) collective-permute-start(f32[8,1,64,512]{3,2,1,0:T(8,128)} %get-tuple-element.11), channel_id=1, source_target_pairs={{16,0},{32,16},{48,32},{64,48},{80,64},{96,80},{112,96},{17,1},{33... | collective-permute-start | bytes 3145736 | tf_op jit(solution)/shard_map/ppermute | solution.py:28
  19.0 66.7 %collective-permute-start.3 = (f32[8,1,64,512]{3,2,1,0:T(8,128)}, f32[8,1,64,512]{3,2,1,0:T(8,128)}, u32[]{:S(2)}, u32[]{:S(2)}) collective-permute-start(f32[8,1,64,512]{3,2,1,0:T(8,128)} %broadcast_in_dim.55), channel_id=1, source_target_pairs={{16,0},{32,16},{48,32},{64,48},{80,64},{96,80},{112,96},{17,1},{33... | collective-permute-start | bytes 3145736 | tf_op jit(solution)/shard_map/ppermute | solution.py:28
  21.4 64.3 %collective-permute-start.2 = (f32[8,1,64,512]{3,2,1,0:T(8,128)}, f32[8,1,64,512]{3,2,1,0:T(8,128)}, u32[]{:S(2)}, u32[]{:S(2)}) collective-permute-start(f32[8,1,64,512]{3,2,1,0:T(8,128)} %broadcast_in_dim.53), channel_id=1, source_target_pairs={{0,16},{16,32},{32,48},{48,64},{64,80},{80,96},{96,112},{1,17},{17... | collective-permute-start | bytes 3145736 | tf_op jit(solution)/shard_map/ppermute | solution.py:25
  34.2 51.6 %copy-start.11 = (f32[2,64,512]{2,1,0:T(8,128)S(1)}, f32[2,64,512]{2,1,0:T(8,128)}, u32[]{:S(2)}) copy-start(f32[2,64,512]{2,1,0:T(8,128)} %param.12) | copy-start | bytes 786436
  86.0 4.7 copy-start.5
  86.0 4.7 copy-start.2
  114.7 75.2 %copy-start.4 = (f32[8,2,64,512]{3,2,1,0:T(8,128)S(1)}, f32[8,2,64,512]{3,2,1,0:T(8,128)}, u32[]{:S(2)}) copy-start(f32[8,2,64,512]{3,2,1,0:T(8,128)} %fusion.72) | copy-start | bytes 6291460
  116.6 44.5 %collective-permute-start.4 = (f32[8,1,64,512]{3,2,1,0:T(8,128)S(1)}, f32[8,1,64,512]{3,2,1,0:T(8,128)S(1)}, u32[]{:S(2)}, u32[]{:S(2)}) collective-permute-start(f32[8,1,64,512]{3,2,1,0:T(8,128)S(1)} %get-tuple-element.8), channel_id=1, source_target_pairs={{0,16},{16,32},{32,48},{48,64},{64,80},{80,96},{96,112},{1,17},{17... | collective-permute-start | bytes 3145736 | tf_op jit(solution)/shard_map/ppermute | solution.py:25
  140.3 48.6 %collective-permute-start.5 = (f32[8,1,64,512]{3,2,1,0:T(8,128)S(1)}, f32[8,1,64,512]{3,2,1,0:T(8,128)S(1)}, u32[]{:S(2)}, u32[]{:S(2)}) collective-permute-start(f32[8,1,64,512]{3,2,1,0:T(8,128)S(1)} %get-tuple-element.9), channel_id=1, source_target_pairs={{16,0},{32,16},{48,32},{64,48},{80,64},{96,80},{112,96},{17,1},{33... | collective-permute-start | bytes 3145736 | tf_op jit(solution)/shard_map/ppermute | solution.py:28
  188.9 1.0 copy-start.9
  217.1 23.7 %collective-permute-start.6 = (f32[8,1,64,512]{3,2,1,0:T(8,128)S(1)}, f32[8,1,64,512]{3,2,1,0:T(8,128)S(1)}, u32[]{:S(2)}, u32[]{:S(2)}) collective-permute-start(f32[8,1,64,512]{3,2,1,0:T(8,128)S(1)} %get-tuple-element.6), channel_id=1, source_target_pairs={{0,16},{16,32},{32,48},{48,64},{64,80},{80,96},{96,112},{1,17},{17... | collective-permute-start | bytes 3145736 | tf_op jit(solution)/shard_map/ppermute | solution.py:25
  220.9 45.6 %collective-permute-start.7 = (f32[8,1,64,512]{3,2,1,0:T(8,128)S(1)}, f32[8,1,64,512]{3,2,1,0:T(8,128)S(1)}, u32[]{:S(2)}, u32[]{:S(2)}) collective-permute-start(f32[8,1,64,512]{3,2,1,0:T(8,128)S(1)} %get-tuple-element.7), channel_id=1, source_target_pairs={{16,0},{32,16},{48,32},{64,48},{80,64},{96,80},{112,96},{17,1},{33... | collective-permute-start | bytes 3145736 | tf_op jit(solution)/shard_map/ppermute | solution.py:28
  222.2 2.5 copy-start.13
  222.2 45.2 %copy-start.3 = (f32[8,2,64,512]{3,2,1,0:T(8,128)S(1)}, f32[8,2,64,512]{3,2,1,0:T(8,128)}, u32[]{:S(2)}) copy-start(f32[8,2,64,512]{3,2,1,0:T(8,128)} %fusion.41) | copy-start | bytes 6291460
  292.9 73.0 %copy-start.6 = (f32[1,8,128,512]{3,1,2,0:T(8,128)S(1)}, f32[1,8,128,512]{3,1,2,0:T(8,128)}, u32[]{:S(2)}) copy-start(f32[1,8,128,512]{3,1,2,0:T(8,128)} %copy.18) | copy-start | bytes 6291460
  367.4 7.8 %copy-start.12 = (f32[8,32]{1,0:T(8,128)S(1)}, f32[8,32]{1,0:T(8,128)}, u32[]{:S(2)}) copy-start(f32[8,32]{1,0:T(8,128)} %param.19) | copy-start | bytes 3076
  367.4 7.8 %copy-start.14 = (f32[32]{0:T(128)S(1)}, f32[32]{0:T(128)}, u32[]{:S(2)}) copy-start(f32[32]{0:T(128)} %param.16) | copy-start | bytes 388
  555.3 2.6 copy-start.1
  (2 other events, 1.7 us)
Sparse Core Ops, SparseCore 0:
  367.5 167.0 all-gather.1
